TPU v7x, 32 devices: a whole 2x2x4 slice. The times are simulated.
32 devices in a mesh: row: 4 (over z), col: 8 (over y, x, core).
Axes of the slice: x: 2, y: 2, z: 4, core: 2. Of those that a mesh axis runs over, the one named last changes fastest.
Arguments:
- points: float32 [16, 1024], P(None, ('row', 'col')), may hold values from -6 to 6
- pivots_first: int32 [128], replicated, may hold values from 0 to 1023, as said below
- pivots_second: int32 [128], replicated, may hold values from 0 to 1023, as said below
Outputs:
- panels: float32 [1024, 256], P('row')
- schur: float32 [1024, 1024], P('row', 'col')
Inputs may be any that keep to these rules, and one draw needn't show every extreme that they name: `pivots_first`: 128 distinct indices, none of them among pivots_second. `pivots_second`: 128 distinct indices, none of them among pivots_first.
All inputs are finite; a program needn't handle non-finite values.
Results may differ from a plain program's by a relative error of at most 0.0003.
Values sent between devices are 32-bit elements; how exact they have to be, the bound alone decides.
No kernel may reach another device: no remote copies, remote signals or barrier semaphores. Data moves between devices by JAX's collectives and lax.ppermute only.
A program may use at most 64 MiB of HBM per device.

v0:
```python
import jax
import jax.numpy as jnp
from jax import lax
from jax.sharding import PartitionSpec as P

DIM = 16
BLOCK = 128


def kernel(left, left_ids, right, right_ids):
    left_sq = jnp.sum(left * left, axis=0)
    right_sq = jnp.sum(right * right, axis=0)
    inner = jnp.dot(left.T, right, precision=lax.Precision.HIGHEST)
    dist = left_sq[:, None] + right_sq[None, :] - 2.0 * inner
    same = (left_ids[:, None] == right_ids[None, :]).astype(jnp.float32)
    return jnp.exp(-dist / DIM) + 0.1 * same


def right_solve(root, columns):
    return jax.scipy.linalg.solve_triangular(root, columns.T, lower=True).T


def per_device(points, pivots_first, pivots_second):
    per_dev = points.shape[1]
    n_row = lax.axis_size("row")
    n_col = lax.axis_size("col")
    row_idx = lax.axis_index("row")
    col_idx = lax.axis_index("col")
    rows_blk = per_dev * n_col
    cols_blk = per_dev * n_row
    row_pts = lax.all_gather(points, "col", axis=1, tiled=True)
    row_ids = row_idx * rows_blk + jnp.arange(rows_blk, dtype=jnp.int32)
    col_ids = col_idx * cols_blk + jnp.arange(cols_blk, dtype=jnp.int32)
    both_pivots = jnp.concatenate([pivots_first, pivots_second])
    everything = lax.all_gather(row_pts, "row", axis=1, tiled=True)
    col_pts = lax.dynamic_slice_in_dim(everything, col_idx * cols_blk, cols_blk, 1)
    pivot_pts = jnp.take(everything, both_pivots, axis=1)
    first_pts = pivot_pts[:, :BLOCK]
    second_pts = pivot_pts[:, BLOCK:]
    first_root = jnp.linalg.cholesky(kernel(first_pts, pivots_first, first_pts, pivots_first))
    first_rows = right_solve(first_root, kernel(row_pts, row_ids, first_pts, pivots_first))
    first_cols = right_solve(first_root, kernel(col_pts, col_ids, first_pts, pivots_first))
    first_pivot = right_solve(
        first_root, kernel(second_pts, pivots_second, first_pts, pivots_first)
    )
    pivot_block = kernel(second_pts, pivots_second, second_pts, pivots_second) - jnp.dot(
        first_pivot, first_pivot.T, precision=lax.Precision.HIGHEST
    )
    second_root = jnp.linalg.cholesky(pivot_block)
    second_rows = kernel(row_pts, row_ids, second_pts, pivots_second) - jnp.dot(
        first_rows, first_pivot.T, precision=lax.Precision.HIGHEST
    )
    second_rows = right_solve(second_root, second_rows)
    second_cols = kernel(col_pts, col_ids, second_pts, pivots_second) - jnp.dot(
        first_cols, first_pivot.T, precision=lax.Precision.HIGHEST
    )
    second_cols = right_solve(second_root, second_cols)
    panel_rows = jnp.concatenate([first_rows, second_rows], axis=1)
    panel_cols = jnp.concatenate([first_cols, second_cols], axis=1)
    schur = kernel(row_pts, row_ids, col_pts, col_ids) - jnp.dot(
        panel_rows, panel_cols.T, precision=lax.Precision.HIGHEST
    )
    return (panel_rows, schur)


def solution(mesh):
    return jax.shard_map(
        per_device,
        mesh=mesh,
        in_specs=(P(None, ("row", "col")), P(), P()),
        out_specs=(P("row", None), P("row", "col")),
        check_vma=False,
    )
```

profile of v0, /device:TPU:0, one launch (start us, length us, event | category | flops | bytes accessed | tf_op | source)
XLA Modules:
  0.0 83.2 jit_solution(11804946262443488814)
XLA Ops:
  0.7 0.6 copy-done.1
  1.4 0.6 copy-done
  2.0 10.7 %all-gather = f32[8,32,16]{1,2,0:T(8,128)S(1)} all-gather(f32[1,32,16]{1,2,0:T(8,128)S(1)} %bitcast.81), channel_id=1, replica_groups=mesh['row'=4,'col'=8] {'col'}, dimensions={0}, use_global_device_ids=true | all-gather | bytes 18432 | tf_op jit(solution)/shard_map/all_gather | solution.py:31
  12.9 16.3 %all_gather.7 = f32[16,1024]{0,1:T(8,128)S(1)} all-gather(f32[16,256]{0,1:T(8,128)S(1)} %bitcast.76), channel_id=1, replica_groups=mesh['row'=4,'col'=8] {'row'}, dimensions={1}, use_global_device_ids=true | all-gather | bytes 81920 | tf_op jit(solution)/shard_map/all_gather | solution.py:35
  29.3 0.7 gather_fusion
  30.3 0.3 fusion.36
  30.7 11.7 %cholesky.44 = f32[128,128]{1,0:T(8,128)S(1)} custom-call(f32[128,128]{1,0:T(8,128)S(1)} %fusion.55), custom_call_target="Cholesky" | custom-call | tf_op jit(solution)/shard_map/jit(cholesky)/cholesky | solution.py:40
  42.4 0.6 compare_reduce_fusion.1
  43.1 0.7 fusion.44
  43.7 9.8 %custom-call.11 = f32[1,128,128]{1,2,0:T(8,128)S(1)} custom-call(f32[1,128,128]{2,1,0:T(8,128)S(1)} %fusion.44), custom_call_target="InvertDiagBlocksLowerTriangular" | custom-call | tf_op jit(solution)/shard_map/jit(_solve_triangular)/triangular_solve | solution.py:20
  54.1 0.3 fusion.15
  55.3 0.3 convolution_subtract_fusion.2
  56.3 11.8 %cholesky.55 = f32[128,128]{1,0:T(8,128)S(1)} custom-call(f32[128,128]{1,0:T(8,128)S(1)} %fusion.48), custom_call_target="Cholesky" | custom-call | tf_op jit(solution)/shard_map/jit(cholesky)/cholesky | solution.py:49
  68.2 0.6 compare_reduce_fusion
  68.8 0.7 fusion.45
  69.5 9.8 %custom-call.13 = f32[1,128,128]{1,2,0:T(8,128)S(1)} custom-call(f32[1,128,128]{2,1,0:T(8,128)S(1)} %fusion.45), custom_call_target="InvertDiagBlocksLowerTriangular" | custom-call | tf_op jit(solution)/shard_map/jit(_solve_triangular)/triangular_solve | solution.py:20
  79.6 0.3 fusion.10
  79.9 0.3 fusion.5
  80.2 0.3 fusion.53
  80.5 0.3 convolution_subtract_fusion.1
  80.8 0.3 convolution_bitcast_fusion
  81.1 0.4 convolution_subtract_fusion
  81.6 0.8 %copy.21 = f32[256,256]{1,0:T(8,128)} copy(f32[256,256]{0,1:T(8,128)S(1)} %pad_maximum_fusion) | data formatting | bytes 524288
  82.4 0.8 copy.22
  (31 shorter events, 3.1 us)
Async XLA Ops:
  0.6 0.7 copy-start.1
  0.7 0.7 copy-start.2
  1.3 0.7 copy-start
where the time goes:
time: 83.4 us; the launch traced here: 83.2 us
  other arithmetic  46.2 us (55%)
  blocking collectives  27.1 us (32%)
  matrix products  5.07 us (6%)
  local copies, waits for them, and re-layouts  3.9 us (5%)
  between operations  0.9 us (1%)
    another operation x4, other arithmetic, right_solve(): return jax.scipy.linalg.solve_triangular(root, columns.T, lower=True).T  20.9 us
    all_gather x1, blocking collectives, per_device(): everything = lax.all_gather(row_pts, 'row', axis=1, tiled=True)  16.3 us
    another operation x3, other arithmetic, per_device(): second_root = jnp.linalg.cholesky(pivot_block)  12.5 us
    another operation x3, other arithmetic, per_device(): jnp.linalg.cholesky(kernel(first_pts, pivots_first, first_pts, pivots_fir...  12.4 us
    all_gather x1, blocking collectives, per_device(): row_pts = lax.all_gather(points, 'col', axis=1, tiled=True)  10.7 us
    unnamed x9, local copies, waits for them, and re-layouts  2.89 us
    dot_general x8, matrix products, kernel(): inner = jnp.dot(left.T, right, precision=lax.Precision.HIGHEST)  2.32 us

commit v1 on v0

v1 whole, which is shorter than its diff:
```python
import functools

import jax
import jax.numpy as jnp
from jax import lax
from jax.experimental import pallas as pl
from jax.experimental.pallas import tpu as pltpu
from jax.sharding import PartitionSpec as P

DIM = 16
LANES = 128
SUB = 8
HALF = 16
PANEL = 32
PER_ROW = LANES // DIM
F32 = jnp.float32
BF16 = jnp.bfloat16
NN = (((1,), (0,)), ((), ()))
NT = (((1,), (1,)), ((), ()))
TN = (((0,), (0,)), ((), ()))


def dot(a, b, dims):
    return lax.dot_general(a, b, dims, preferred_element_type=F32)


def split2(a):
    hi = a.astype(BF16)
    return hi, (a - hi.astype(F32)).astype(BF16)


def split3(a):
    hi = a.astype(BF16)
    rest = a - hi.astype(F32)
    mid = rest.astype(BF16)
    return hi, mid, (rest - mid.astype(F32)).astype(BF16)


def dot_f32(a, b, dims):
    a_hi, a_lo = split2(a)
    b_hi, b_lo = split2(b)
    return dot(a_hi, b_hi, dims) + (dot(a_hi, b_lo, dims) + dot(a_lo, b_hi, dims))


def dot6(a, b, dims):
    a0, a1, a2 = split3(a)
    b0, b1, b2 = split3(b)
    return dot(a0, b0, dims) + ((dot(a0, b1, dims) + dot(a1, b0, dims)) + (dot(a1, b1, dims) + (dot(a0, b2, dims) + dot(a2, b0, dims))))

def exp_dist(left, right):
    left_sq = jnp.sum(left * left, axis=1, keepdims=True)
    ones = jnp.ones((SUB, DIM), F32)
    right_sq = lax.dot_general(ones, right * right, NT, precision=lax.Precision.HIGHEST, preferred_element_type=F32)[:1]
    inner = lax.dot_general(left, right, NT, precision=lax.Precision.HIGHEST, preferred_element_type=F32)
    return jnp.exp((left_sq + right_sq - 2.0 * inner) * (-1.0 / DIM))


def unpack_points(table, select, segment):
    n = segment.shape[0]
    lane = lax.broadcasted_iota(jnp.int32, (n, LANES), 1)
    keep = (lane // DIM) == segment
    fold = (lax.broadcasted_iota(jnp.int32, (LANES, DIM), 0) % DIM == lax.broadcasted_iota(jnp.int32, (LANES, DIM), 1)).astype(BF16)
    total = None
    for part in split3(table):
        row = dot(select, part, NN)
        x = dot(jnp.where(keep, row, 0.0).astype(BF16), fold, NN)
        total = x if total is None else total + x
    return total


def run_points(table_ref, start, count):
    rows = count // PER_ROW
    table = table_ref[pl.ds(pl.multiple_of(start // PER_ROW, SUB), rows), :]
    ids = lax.broadcasted_iota(jnp.int32, (count, rows), 0)
    select = (ids // PER_ROW == lax.broadcasted_iota(jnp.int32, (count, rows), 1)).astype(BF16)
    segment = lax.broadcasted_iota(jnp.int32, (count, 1), 0) % PER_ROW
    return unpack_points(table, select, segment)


def row_of(tile, s):
    return jnp.broadcast_to(tile[s : s + 1, :], (SUB, LANES))


def eliminate(rows, first_lane, n_tiles):
    sub = lax.broadcasted_iota(jnp.int32, (SUB, LANES), 0)
    lane = lax.broadcasted_iota(jnp.int32, (SUB, LANES), 1)
    at, off = first_lane // LANES, first_lane % LANES
    n_lt = len(rows[0])
    cols = [
        [jnp.broadcast_to(rows[i][at][:, off + j : off + j + 1], (SUB, LANES)) if i >= j // SUB else None for i in range(n_tiles)]
        for j in range(HALF)
    ]
    own = (lane >= off) & (lane < off + HALF)
    for i in range(n_tiles):
        unit = (lane == off + i * SUB + sub).astype(F32) if i < 2 else jnp.zeros((SUB, LANES), F32)
        rows[i][at] = jnp.where(own, unit, rows[i][at])
    scaled = []
    for it in range(2):
        shift = jnp.zeros((SUB, LANES), F32)
        scale = jnp.zeros((SUB, LANES), F32)
        for sl in range(0, SUB, 2):
            s = it * SUB + sl
            a = row_of(cols[s][it], sl)
            b = row_of(cols[s][it], sl + 1)
            c = row_of(cols[s + 1][it], sl + 1)
            det = a * c - b * b
            rdet = 1.0 / det
            ra = lax.rsqrt(a)
            ba = b * (ra * ra)
            rc = lax.rsqrt(c - b * ba)
            scale = jnp.where(sub == sl, ra, jnp.where(sub == sl + 1, rc, scale))
            shift = jnp.where(sub == sl + 1, ba, shift)
            begin = it if sl + 2 < SUB else it + 1
            m0, m1 = [None] * n_tiles, [None] * n_tiles
            for i in range(begin, n_tiles):
                u0, u1 = cols[s][i], cols[s + 1][i]
                m0[i] = (u0 * c - u1 * b) * rdet
                m1[i] = (u1 * a - u0 * b) * rdet
                if i == it:
                    m0[i] = jnp.where(sub > sl + 1, m0[i], 0.0)
                    m1[i] = jnp.where(sub > sl + 1, m1[i], 0.0)
            for j in range(s + 2, HALF):
                x0 = row_of(cols[s][j // SUB], j % SUB)
                x1 = row_of(cols[s + 1][j // SUB], j % SUB)
                for i in range(max(begin, j // SUB), n_tiles):
                    cols[j][i] = cols[j][i] - (m0[i] * x0 + m1[i] * x1)
            for t in range(n_lt):
                y0 = row_of(rows[it][t], sl)
                y1 = row_of(rows[it][t], sl + 1)
                for i in range(begin, n_tiles):
                    rows[i][t] = rows[i][t] - (m0[i] * y0 + m1[i] * y1)
        scaled.append([(r - shift * pltpu.roll(r, 1, 0)) * scale for r in rows[it]])
    return scaled, rows[2:]


def inverse_factor(w_ref, x_ref, n):
    n_lt = n // LANES
    lane = lax.broadcasted_iota(jnp.int32, (SUB, LANES), 1)
    for r in range(0, n, PANEL):
        rows = [[w_ref[r + i * SUB : r + (i + 1) * SUB, t * LANES : (t + 1) * LANES] for t in range(n_lt)] for i in range(PANEL // SUB)]
        upper, lower = eliminate(rows, r, 4)
        lower, _ = eliminate(lower, r + HALF, 2)
        at, off = r // LANES, r % LANES
        other = (lane >= off + HALF) & (lane < off + PANEL)
        for i in range(2):
            upper[i][at] = jnp.where(other, 0.0, upper[i][at])
        done = upper + lower
        for i in range(PANEL // SUB):
            for t in range(n_lt):
                tile = done[i][t]
                if t > at:
                    tile = jnp.zeros((SUB, LANES), F32)
                elif t == at:
                    tile = jnp.where(lane >= off + PANEL, 0.0, tile)
                x_ref[r + i * SUB : r + (i + 1) * SUB, t * LANES : (t + 1) * LANES] = tile
        nxt = r + PANEL
        if nxt == n:
            break
        whole = jnp.concatenate([jnp.concatenate(t, axis=1) for t in done], axis=0)
        base = nxt // LANES * LANES
        hi, lo = split2(whole)
        left = jnp.concatenate([hi, hi, lo], axis=0)[:, base:]
        right = jnp.concatenate([hi, lo, hi], axis=0)
        update = dot6(whole[:, base:], whole, TN)[nxt - base :, :]
        wide = lax.broadcasted_iota(jnp.int32, (n - nxt, n), 1)
        w_ref[nxt:, :] = jnp.where((wide >= r) & (wide < nxt), 0.0, w_ref[nxt:, :]) - update


def per_device_kernel(chunk, cols_n, table_ref, pivots_ref, panels_ref, schur_ref, w_ref, x_ref):
    row_start = lax.axis_index("row") * panels_ref.shape[0]
    col_start = lax.axis_index("col") * cols_n
    n_piv = w_ref.shape[0]
    n_tab = table_ref.shape[0]
    lane_ids = pivots_ref[...]
    ids = jnp.concatenate(
        [jnp.broadcast_to(lane_ids[i : i + 1, :].astype(F32), (LANES, LANES)).T for i in range(n_piv // LANES)], axis=0
    ).astype(jnp.int32)
    select = jnp.concatenate(
        [(ids // PER_ROW == t * LANES + lax.broadcasted_iota(jnp.int32, (n_piv, LANES), 1)).astype(BF16) for t in range(n_tab // LANES)],
        axis=1,
    )
    piv = unpack_points(table_ref[...], select, ids[:, :1] % PER_ROW)
    own = lax.broadcasted_iota(jnp.int32, (n_piv, n_piv), 0) == lax.broadcasted_iota(jnp.int32, (n_piv, n_piv), 1)
    w_ref[...] = exp_dist(piv, piv) + jnp.where(own, 0.1, 0.0)
    inverse_factor(w_ref, x_ref, n_piv)
    x_hi, x_lo = split2(x_ref[...])
    piv_row = jnp.concatenate([lane_ids[i : i + 1, :] for i in range(n_piv // LANES)], axis=1)

    def panel_of(start, count):
        pts = run_points(table_ref, start, count)
        ids_here = start + lax.broadcasted_iota(jnp.int32, (count, n_piv), 0)
        c = exp_dist(pts, piv) + jnp.where(ids_here == piv_row, 0.1, 0.0)
        c_hi, c_lo = split2(c)
        return pts, dot6(c, x_ref[...], NT)

    col_pts, col_panel = panel_of(col_start, cols_n)
    c_hi, c_lo = split2(col_panel)

    def one_chunk(at):
        start = row_start + at
        pts, panel = panel_of(start, chunk)
        panels_ref[pl.ds(at, chunk), :] = panel
        p_hi, p_lo = split2(panel)
        low = dot6(panel, col_panel, NT)
        ids_row = start + lax.broadcasted_iota(jnp.int32, (chunk, cols_n), 0)
        ids_col = col_start + lax.broadcasted_iota(jnp.int32, (chunk, cols_n), 1)
        schur_ref[pl.ds(at, chunk), :] = exp_dist(pts, col_pts) + jnp.where(ids_row == ids_col, 0.1, 0.0) - low

    n_rows = panels_ref.shape[0]
    if n_rows == chunk:
        one_chunk(0)
    else:

        @pl.loop(0, n_rows // chunk)
        def _(i):
            one_chunk(pl.multiple_of(i * chunk, chunk))


def per_device(points, pivots_first, pivots_second):
    per_dev = points.shape[1]
    n_row = lax.axis_size("row")
    n_col = lax.axis_size("col")
    rows_n = per_dev * n_col
    cols_n = per_dev * n_row
    n_piv = pivots_first.shape[0] + pivots_second.shape[0]
    packed = points.T.reshape(per_dev * DIM // LANES, LANES)
    table = lax.all_to_all(jnp.tile(packed, (n_row * n_col, 1)), ("row", "col"), 0, 0, tiled=True)
    pivots = jnp.concatenate([pivots_first, pivots_second]).reshape(n_piv // LANES, LANES)
    chunk = min(rows_n, 256)
    return pl.pallas_call(
        functools.partial(per_device_kernel, chunk, cols_n),
        out_shape=(jax.ShapeDtypeStruct((rows_n, n_piv), F32), jax.ShapeDtypeStruct((rows_n, cols_n), F32)),
        in_specs=[pl.BlockSpec(memory_space=pltpu.VMEM)] * 2,
        out_specs=(pl.BlockSpec(memory_space=pltpu.VMEM),) * 2,
        scratch_shapes=[pltpu.VMEM((n_piv, n_piv), F32)] * 2,
        name="pivoted_cholesky",
    )(table, pivots)


def solution(mesh):
    return jax.shard_map(
        per_device,
        mesh=mesh,
        in_specs=(P(None, ("row", "col")), P(), P()),
        out_specs=(P("row", None), P("row", "col")),
        check_vma=False,
    )
```

time: 83.4 us -> 29.4 us (0.35)
  other arithmetic: 46.2 us -> 0.59 us
  blocking collectives: 27.1 us -> 0 us
  Pallas kernels: 0 us -> 11.6 us
  starting transfers between devices: 0 us -> 7.33 us
  waiting for transfers between devices: 0 us -> 6.8 us
  matrix products: 5.07 us -> 0 us
  local copies, waits for them, and re-layouts: 3.9 us -> 2.12 us
    another operation x10 -> x0, other arithmetic: 45.8 us -> none  [the longest x4 20.9 us: right_solve(): return jax.scipy.linalg.solve_triangular(root, columns.T, lower=True).T]
    all_gather x2 -> x0, blocking collectives: 27.1 us -> none  [the longest x1 16.3 us: per_device(): everything = lax.all_gather(row_pts, 'row', axis=1, tiled=True)]
    pallas_call x0 -> x1, Pallas kernels: none -> 11.6 us  [per_device(): pl.pallas_call(functools.partial(per_device_kernel, chunk, cols_n), out_s...]
    all_to_all x0 -> x1, starting transfers between devices: none -> 7.33 us  [per_device(): lax.all_to_all(jnp.tile(packed, (n_row * n_col, 1)), ('row', 'col'), 0, 0...]
    all_to_all x0 -> x1, waiting for transfers between devices: none -> 6.8 us  [per_device(): lax.all_to_all(jnp.tile(packed, (n_row * n_col, 1)), ('row', 'col'), 0, 0...]
    dot_general x12 -> x0, matrix products: 3.61 us -> none  [the longest x8 2.32 us: kernel(): inner = jnp.dot(left.T, right, precision=lax.Precision.HIGHEST)]
    unnamed x9 -> x6, local copies, waits for them, and re-layouts: 2.89 us -> 0.63 us
    another operation x5 -> x0, matrix products: 1.47 us -> none  [right_solve(): return jax.scipy.linalg.solve_triangular(root, columns.T, lower=True).T]
  transfers between devices with their start and end apart: 0 -> 1, of which waited for: 0 -> 1; matrix products, arithmetic and copies ran while one was open for 0% -> 2% of each run, Pallas kernels for 0% -> 0%
where the time goes in v1:
time: 29.4 us; the launch traced here: 29.1 us
  Pallas kernels  11.6 us (39%)
  starting transfers between devices  7.33 us (25%)
  waiting for transfers between devices  6.8 us (23%)
  local copies, waits for them, and re-layouts  2.12 us (7%)
  between operations  0.66 us (2%)
  other arithmetic  0.59 us (2%)
    pallas_call x1, Pallas kernels, per_device(): pl.pallas_call(functools.partial(per_device_kernel, chunk, cols_n), out_s...  11.6 us
    all_to_all x1, starting transfers between devices, per_device(): lax.all_to_all(jnp.tile(packed, (n_row * n_col, 1)), ('row', 'col'), 0, 0...  7.33 us
    all_to_all x1, waiting for transfers between devices, per_device(): lax.all_to_all(jnp.tile(packed, (n_row * n_col, 1)), ('row', 'col'), 0, 0...  6.8 us
    transpose x1, local copies, waits for them, and re-layouts, per_device(): packed = points.T.reshape(per_dev * DIM // LANES, LANES)  0.77 us
    another operation x2, local copies, waits for them, and re-layouts, per_device(): jnp.tile(packed, (n_row * n_col, 1))  0.73 us
    unnamed x6, local copies, waits for them, and re-layouts  0.63 us
  transfers between devices with their start and end apart: 1, of which 1 were waited for; matrix products, arithmetic and copies ran while one was open for 2% of the time, Pallas kernels for 0%

profile of v1, /device:TPU:0, one launch (start us, length us, event | category | flops | bytes accessed | tf_op | source)
XLA Modules:
  0.0 29.1 jit_solution(5758839533059103768)
XLA Ops:
  0.6 0.8 %copy.5 = f32[32,16]{1,0:T(8,128)S(1)} copy(f32[32,16]{0,1:T(8,128)} %bitcast.5) | data formatting | bytes 4096 | tf_op jit(solution)/shard_map/transpose | solution.py:226
  1.4 0.1 tile.8
  1.5 0.6 %tile.9 = f32[32,4,128]{2,1,0:T(4,128)} broadcast(f32[4,128]{1,0:T(4,128)S(1)} %tile.8), dimensions={1,2} | broadcast | bytes 67584 | tf_op jit(solution)/shard_map/tile | solution.py:227
  2.1 0.0 copy-start.1
  2.1 0.0 copy-start.2
  2.1 7.3 %all-to-all-start = ((f32[32,4,128]{2,1,0:T(4,128)}), f32[32,4,128]{2,1,0:T(4,128)S(1)}, u32[]{:S(2)}, u32[]{:S(2)}) async-start(f32[32,4,128]{2,1,0:T(4,128)} %tile.9), calls=%async_computation | async-start | bytes 131072 | tf_op jit(solution)/shard_map/all_to_all | solution.py:227
  9.5 0.0 copy-done.1
  9.5 0.0 copy-done.2
  9.5 0.6 %add_bitcast_fusion.pivots_ref = s32[2,128]{1,0:T(2,128)} fusion(s32[128]{0:T(128)S(1)} %copy-done.1, s32[128]{0:T(128)S(1)} %copy-done.2), kind=kLoop, calls=%fused_computation | loop fusion | flops 256 | bytes 2048 | tf_op jit(solution)/shard_map/reshape | solution.py:228
  10.1 6.8 %all-to-all-done = f32[32,4,128]{2,1,0:T(4,128)S(1)} async-done(((f32[32,4,128]{2,1,0:T(4,128)}), f32[32,4,128]{2,1,0:T(4,128)S(1)}, u32[]{:S(2)}, u32[]{:S(2)}) %all-to-all-start) | async-done | bytes 65568 | tf_op jit(solution)/shard_map/all_to_all | solution.py:227
  16.9 0.0 copy-start
  16.9 0.6 %copy-done = f32[32,4,128]{2,1,0:T(4,128)} copy-done((f32[32,4,128]{2,1,0:T(4,128)}, f32[32,4,128]{2,1,0:T(4,128)S(1)}, u32[]{:S(2)}) %copy-start) | copy-done | bytes 65560
  17.5 11.6 %pivoted_cholesky.1 = (f32[256,256]{1,0:T(8,128)}, f32[256,128]{1,0:T(8,128)}) custom-call(f32[128,128]{1,0:T(8,128)} %bitcast.4, s32[2,128]{1,0:T(2,128)} %add_bitcast_fusion.pivots_ref), custom_call_target="tpu_custom_call" | custom-call | tf_op jit(solution)/shard_map/pivoted_cholesky/pallas_call | solution.py:230
Async XLA Ops:
  2.1 7.3 %copy-start.1 = (s32[128]{0:T(128)S(1)}, s32[128]{0:T(128)}, u32[]{:S(2)}) copy-start(s32[128]{0:T(128)} %param.5) | copy-start | bytes 1540
  2.1 7.3 %copy-start.2 = (s32[128]{0:T(128)S(1)}, s32[128]{0:T(128)}, u32[]{:S(2)}) copy-start(s32[128]{0:T(128)} %param.4) | copy-start | bytes 1540
  2.1 14.7 %all-to-all-start = ((f32[32,4,128]{2,1,0:T(4,128)}), f32[32,4,128]{2,1,0:T(4,128)S(1)}, u32[]{:S(2)}, u32[]{:S(2)}) async-start(f32[32,4,128]{2,1,0:T(4,128)} %tile.9), calls=%async_computation | async-start | bytes 131072 | tf_op jit(solution)/shard_map/all_to_all | solution.py:227
  16.9 0.6 %copy-start = (f32[32,4,128]{2,1,0:T(4,128)}, f32[32,4,128]{2,1,0:T(4,128)S(1)}, u32[]{:S(2)}) copy-start(f32[32,4,128]{2,1,0:T(4,128)S(1)} %all-to-all-done) | copy-start | bytes 196612

commit v2 on v1

--- a/solution.py
+++ b/solution.py
@@ -13,6 +13,7 @@
 HALF = 16
 PANEL = 32
 PER_ROW = LANES // DIM
+VMEM_BYTES = 24 * 2**20
 F32 = jnp.float32
 BF16 = jnp.bfloat16
 NN = (((1,), (0,)), ((), ()))
@@ -24,22 +25,11 @@
     return lax.dot_general(a, b, dims, preferred_element_type=F32)
 
 
-def split2(a):
-    hi = a.astype(BF16)
-    return hi, (a - hi.astype(F32)).astype(BF16)
-
-
 def split3(a):
     hi = a.astype(BF16)
     rest = a - hi.astype(F32)
     mid = rest.astype(BF16)
     return hi, mid, (rest - mid.astype(F32)).astype(BF16)
-
-
-def dot_f32(a, b, dims):
-    a_hi, a_lo = split2(a)
-    b_hi, b_lo = split2(b)
-    return dot(a_hi, b_hi, dims) + (dot(a_hi, b_lo, dims) + dot(a_lo, b_hi, dims))
 
 
 def dot6(a, b, dims):
@@ -87,15 +77,18 @@
     at, off = first_lane // LANES, first_lane % LANES
     n_lt = len(rows[0])
     cols = [
-        [jnp.broadcast_to(rows[i][at][:, off + j : off + j + 1], (SUB, LANES)) if i >= j // SUB else None for i in range(n_tiles)]
+        [
+            jnp.broadcast_to(jnp.sum(jnp.where(lane == off + j, rows[i][at], 0.0), axis=1, keepdims=True), (SUB, LANES)) if i >= j // SUB else None
+            for i in range(n_tiles)
+        ]
         for j in range(HALF)
     ]
     own = (lane >= off) & (lane < off + HALF)
     for i in range(n_tiles):
-        unit = (lane == off + i * SUB + sub).astype(F32) if i < 2 else jnp.zeros((SUB, LANES), F32)
+        unit = (lane == off + i * SUB + sub).astype(F32) if i < HALF // SUB else jnp.zeros((SUB, LANES), F32)
         rows[i][at] = jnp.where(own, unit, rows[i][at])
     scaled = []
-    for it in range(2):
+    for it in range(HALF // SUB):
         shift = jnp.zeros((SUB, LANES), F32)
         scale = jnp.zeros((SUB, LANES), F32)
         for sl in range(0, SUB, 2):
@@ -130,7 +123,7 @@
                 for i in range(begin, n_tiles):
                     rows[i][t] = rows[i][t] - (m0[i] * y0 + m1[i] * y1)
         scaled.append([(r - shift * pltpu.roll(r, 1, 0)) * scale for r in rows[it]])
-    return scaled, rows[2:]
+    return scaled, rows[HALF // SUB :]
 
 
 def inverse_factor(w_ref, x_ref, n):
@@ -138,13 +131,14 @@
     lane = lax.broadcasted_iota(jnp.int32, (SUB, LANES), 1)
     for r in range(0, n, PANEL):
         rows = [[w_ref[r + i * SUB : r + (i + 1) * SUB, t * LANES : (t + 1) * LANES] for t in range(n_lt)] for i in range(PANEL // SUB)]
-        upper, lower = eliminate(rows, r, 4)
-        lower, _ = eliminate(lower, r + HALF, 2)
         at, off = r // LANES, r % LANES
-        other = (lane >= off + HALF) & (lane < off + PANEL)
-        for i in range(2):
-            upper[i][at] = jnp.where(other, 0.0, upper[i][at])
-        done = upper + lower
+        done = []
+        for begin in range(0, PANEL, HALF):
+            upper, rows = eliminate(rows, r + begin, len(rows))
+            other = (lane >= off + begin + HALF) & (lane < off + PANEL)
+            for tiles in upper:
+                tiles[at] = jnp.where(other, 0.0, tiles[at])
+            done += upper
         for i in range(PANEL // SUB):
             for t in range(n_lt):
                 tile = done[i][t]
@@ -158,12 +152,17 @@
             break
         whole = jnp.concatenate([jnp.concatenate(t, axis=1) for t in done], axis=0)
         base = nxt // LANES * LANES
-        hi, lo = split2(whole)
-        left = jnp.concatenate([hi, hi, lo], axis=0)[:, base:]
-        right = jnp.concatenate([hi, lo, hi], axis=0)
-        update = dot6(whole[:, base:], whole, TN)[nxt - base :, :]
-        wide = lax.broadcasted_iota(jnp.int32, (n - nxt, n), 1)
-        w_ref[nxt:, :] = jnp.where((wide >= r) & (wide < nxt), 0.0, w_ref[nxt:, :]) - update
+        r0, r1, r2 = split3(whole)
+        left = jnp.concatenate([r0, r0, r1, r1, r0, r2], axis=0)[:, base:].T
+        right = jnp.concatenate([r0, r1, r0, r1, r2, r0], axis=0)
+        wide = lax.broadcasted_iota(jnp.int32, (PANEL, n), 1)
+        mid = nxt + PANEL
+        update = dot(left[nxt - base : mid - base, :], right, NN)
+        w_ref[nxt:mid, :] = jnp.where((wide >= r) & (wide < nxt), 0.0, w_ref[nxt:mid, :]) - update
+        if mid < n:
+            wide = lax.broadcasted_iota(jnp.int32, (n - mid, n), 1)
+            update = dot(left[mid - base :, :], right, NN)
+            w_ref[mid:, :] = jnp.where((wide >= r) & (wide < nxt), 0.0, w_ref[mid:, :]) - update
 
 
 def per_device_kernel(chunk, cols_n, table_ref, pivots_ref, panels_ref, schur_ref, w_ref, x_ref):
@@ -171,6 +170,7 @@
     col_start = lax.axis_index("col") * cols_n
     n_piv = w_ref.shape[0]
     n_tab = table_ref.shape[0]
+    n_rows = panels_ref.shape[0]
     lane_ids = pivots_ref[...]
     ids = jnp.concatenate(
         [jnp.broadcast_to(lane_ids[i : i + 1, :].astype(F32), (LANES, LANES)).T for i in range(n_piv // LANES)], axis=0
@@ -182,38 +182,43 @@
     piv = unpack_points(table_ref[...], select, ids[:, :1] % PER_ROW)
     own = lax.broadcasted_iota(jnp.int32, (n_piv, n_piv), 0) == lax.broadcasted_iota(jnp.int32, (n_piv, n_piv), 1)
     w_ref[...] = exp_dist(piv, piv) + jnp.where(own, 0.1, 0.0)
-    inverse_factor(w_ref, x_ref, n_piv)
-    x_hi, x_lo = split2(x_ref[...])
     piv_row = jnp.concatenate([lane_ids[i : i + 1, :] for i in range(n_piv // LANES)], axis=1)
 
-    def panel_of(start, count):
+    def columns_of(start, count):
         pts = run_points(table_ref, start, count)
         ids_here = start + lax.broadcasted_iota(jnp.int32, (count, n_piv), 0)
-        c = exp_dist(pts, piv) + jnp.where(ids_here == piv_row, 0.1, 0.0)
-        c_hi, c_lo = split2(c)
-        return pts, dot6(c, x_ref[...], NT)
-
-    col_pts, col_panel = panel_of(col_start, cols_n)
-    c_hi, c_lo = split2(col_panel)
-
-    def one_chunk(at):
+        return pts, exp_dist(pts, piv) + jnp.where(ids_here == piv_row, 0.1, 0.0)
+
+    col_pts, col_columns = columns_of(col_start, cols_n)
+
+    def prepare(at):
         start = row_start + at
-        pts, panel = panel_of(start, chunk)
-        panels_ref[pl.ds(at, chunk), :] = panel
-        p_hi, p_lo = split2(panel)
-        low = dot6(panel, col_panel, NT)
+        pts, columns = columns_of(start, chunk)
         ids_row = start + lax.broadcasted_iota(jnp.int32, (chunk, cols_n), 0)
         ids_col = col_start + lax.broadcasted_iota(jnp.int32, (chunk, cols_n), 1)
-        schur_ref[pl.ds(at, chunk), :] = exp_dist(pts, col_pts) + jnp.where(ids_row == ids_col, 0.1, 0.0) - low
-
-    n_rows = panels_ref.shape[0]
+        return columns, exp_dist(pts, col_pts) + jnp.where(ids_row == ids_col, 0.1, 0.0)
+
+    def finish(at, columns, k_cols, x, col_panel):
+        panel = dot6(columns, x, NT)
+        panels_ref[pl.ds(at, chunk), :] = panel
+        schur_ref[pl.ds(at, chunk), :] = k_cols - dot6(panel, col_panel, NT)
+
     if n_rows == chunk:
-        one_chunk(0)
+        inverse_factor(w_ref, x_ref, n_piv)
+        columns, k_cols = prepare(0)
+        x = x_ref[...]
+        both = dot6(jnp.concatenate([columns, col_columns], axis=0), x, NT)
+        panels_ref[...] = both[:chunk]
+        schur_ref[...] = k_cols - dot6(both[:chunk], both[chunk:], NT)
     else:
+        inverse_factor(w_ref, x_ref, n_piv)
+        col_panel = dot6(col_columns, x_ref[...], NT)
 
         @pl.loop(0, n_rows // chunk)
         def _(i):
-            one_chunk(pl.multiple_of(i * chunk, chunk))
+            at = pl.multiple_of(i * chunk, chunk)
+            columns, k_cols = prepare(at)
+            finish(at, columns, k_cols, x_ref[...], col_panel)
 
 
 def per_device(points, pivots_first, pivots_second):
@@ -233,6 +238,7 @@
         in_specs=[pl.BlockSpec(memory_space=pltpu.VMEM)] * 2,
         out_specs=(pl.BlockSpec(memory_space=pltpu.VMEM),) * 2,
         scratch_shapes=[pltpu.VMEM((n_piv, n_piv), F32)] * 2,
+        compiler_params=pltpu.CompilerParams(vmem_limit_bytes=VMEM_BYTES),
         name="pivoted_cholesky",
     )(table, pivots)
 

time: 29.4 us -> 25.5 us (0.87)
  Pallas kernels: 11.6 us -> 8.34 us
  local copies, waits for them, and re-layouts: 2.12 us -> 1.51 us
  other arithmetic: 0.59 us -> 0.01 us
  waiting for transfers between devices: 6.8 us -> 7.37 us
    pallas_call x1, Pallas kernels: 11.6 us -> 8.34 us  [per_device(): pl.pallas_call(functools.partial(per_device_kernel, chunk, cols_n), out_s...]
    unnamed x6 -> x4, local copies, waits for them, and re-layouts: 0.63 us -> 0.01 us
    reshape x1, other arithmetic: 0.59 us -> 0.01 us  [per_device(): jnp.concatenate([pivots_first, pivots_second])]
    all_to_all x1, waiting for transfers between devices: 6.8 us -> 7.37 us  [per_device(): lax.all_to_all(jnp.tile(packed, (n_row * n_col, 1)), ('row', 'col'), 0, 0...]
  transfers between devices with their start and end apart: 1 -> 1, of which waited for: 1 -> 1; matrix products, arithmetic and copies ran while one was open for 2% -> 0% of each run, Pallas kernels for 0% -> 0%
where the time goes in v2:
time: 25.5 us; the launch traced here: 25.2 us
  Pallas kernels  8.34 us (33%)
  waiting for transfers between devices  7.37 us (29%)
  starting transfers between devices  7.33 us (29%)
  local copies, waits for them, and re-layouts  1.51 us (6%)
  between operations  0.66 us (3%)
    pallas_call x1, Pallas kernels, per_device(): pl.pallas_call(functools.partial(per_device_kernel, chunk, cols_n), out_s...  8.34 us
    all_to_all x1, waiting for transfers between devices, per_device(): lax.all_to_all(jnp.tile(packed, (n_row * n_col, 1)), ('row', 'col'), 0, 0...  7.37 us
    all_to_all x1, starting transfers between devices, per_device(): lax.all_to_all(jnp.tile(packed, (n_row * n_col, 1)), ('row', 'col'), 0, 0...  7.33 us
    transpose x1, local copies, waits for them, and re-layouts, per_device(): packed = points.T.reshape(per_dev * DIM // LANES, LANES)  0.77 us
    another operation x2, local copies, waits for them, and re-layouts, per_device(): jnp.tile(packed, (n_row * n_col, 1))  0.73 us
  transfers between devices with their start and end apart: 1, of which 1 were waited for; matrix products, arithmetic and copies ran while one was open for 0% of the time, Pallas kernels for 0%

profile of v2, /device:TPU:0, one launch (start us, length us, event | category | flops | bytes accessed | tf_op | source)
XLA Modules:
  0.0 25.2 jit_solution(17150755513839955444)
XLA Ops:
  0.6 0.8 %copy.5 = f32[32,16]{1,0:T(8,128)S(1)} copy(f32[32,16]{0,1:T(8,128)} %bitcast.5) | data formatting | bytes 4096 | tf_op jit(solution)/shard_map/transpose | solution.py:231
  1.4 0.1 tile.8
  1.5 0.6 %tile.9 = f32[32,4,128]{2,1,0:T(4,128)} broadcast(f32[4,128]{1,0:T(4,128)S(1)} %tile.8), dimensions={1,2} | broadcast | bytes 67584 | tf_op jit(solution)/shard_map/tile | solution.py:232
  2.1 0.0 copy-start
  2.1 0.0 copy-start.1
  2.1 7.3 %all-to-all-start = ((f32[32,4,128]{2,1,0:T(4,128)}), f32[32,4,128]{2,1,0:T(4,128)S(1)}, u32[]{:S(2)}, u32[]{:S(2)}) async-start(f32[32,4,128]{2,1,0:T(4,128)} %tile.9), calls=%async_computation | async-start | bytes 131072 | tf_op jit(solution)/shard_map/all_to_all | solution.py:232
  9.5 0.0 copy-done
  9.5 0.0 copy-done.1
  9.5 7.4 %all-to-all-done = f32[32,4,128]{2,1,0:T(4,128)S(1)} async-done(((f32[32,4,128]{2,1,0:T(4,128)}), f32[32,4,128]{2,1,0:T(4,128)S(1)}, u32[]{:S(2)}, u32[]{:S(2)}) %all-to-all-start) | async-done | bytes 65568 | tf_op jit(solution)/shard_map/all_to_all | solution.py:232
  16.9 8.3 %pivoted_cholesky.1 = (f32[256,256]{1,0:T(8,128)}, f32[256,128]{1,0:T(8,128)}) custom-call(f32[128,128]{1,0:T(8,128)S(1)} %bitcast.4, s32[2,128]{1,0:T(2,128)S(1)} %add_bitcast_fusion.pivots_ref), custom_call_target="tpu_custom_call" | custom-call | tf_op jit(solution)/shard_map/pivoted_cholesky/pallas_call | solution.py:235
  (1 shorter events, 0.0 us)
Async XLA Ops:
  2.1 7.3 %copy-start = (s32[128]{0:T(128)S(1)}, s32[128]{0:T(128)}, u32[]{:S(2)}) copy-start(s32[128]{0:T(128)} %param.5) | copy-start | bytes 1540
  2.1 7.3 %copy-start.1 = (s32[128]{0:T(128)S(1)}, s32[128]{0:T(128)}, u32[]{:S(2)}) copy-start(s32[128]{0:T(128)} %param.4) | copy-start | bytes 1540
  2.1 14.7 %all-to-all-start = ((f32[32,4,128]{2,1,0:T(4,128)}), f32[32,4,128]{2,1,0:T(4,128)S(1)}, u32[]{:S(2)}, u32[]{:S(2)}) async-start(f32[32,4,128]{2,1,0:T(4,128)} %tile.9), calls=%async_computation | async-start | bytes 131072 | tf_op jit(solution)/shard_map/all_to_all | solution.py:232

commit v3 on v0

v3 whole, which is shorter than its diff:
```python
import functools

import jax
import jax.numpy as jnp
from jax import lax
from jax.experimental import pallas as pl
from jax.experimental.pallas import tpu as pltpu
from jax.sharding import PartitionSpec as P

DIM = 16
LANES = 128
SUB = 8
BLOCK = 16
PER_ROW = LANES // DIM
VMEM_BYTES = 24 * 2**20
F32 = jnp.float32
BF16 = jnp.bfloat16
NN = (((1,), (0,)), ((), ()))
NT = (((1,), (1,)), ((), ()))
TN = (((0,), (0,)), ((), ()))
LEFT = (0, 0, 1, 1, 0, 2)
RIGHT = (0, 1, 0, 1, 2, 0)
NORM = len(LEFT) * DIM


def iota(shape, axis):
    return lax.broadcasted_iota(jnp.int32, shape, axis)


def dot(a, b, dims):
    return lax.dot_general(a, b, dims, preferred_element_type=F32)


def split3(a):
    hi = a.astype(BF16)
    rest = a - hi.astype(F32)
    mid = rest.astype(BF16)
    return hi, mid, (rest - mid.astype(F32)).astype(BF16)


def dot6(a, b, dims):
    p = [dot(a[i], b[j], dims) for i, j in zip(LEFT, RIGHT)]
    return p[0] + ((p[1] + p[2]) + ((p[3] + p[4]) + p[5]))


def pack_kernel(points_in, first_in, second_in, table_ref, select_ref, keep_ref, ids_ref, place_ref, points_ref, first_ref, second_ref, sems):
    copies = [
        pltpu.make_async_copy(src, dst, sems.at[i])
        for i, (src, dst) in enumerate(((points_in, points_ref), (first_in, first_ref), (second_in, second_ref)))
    ]
    for copy in copies:
        copy.start()
    lane = iota((LANES, LANES), 1)
    same = lane % DIM == iota((LANES, LANES), 0) % DIM
    for third in range(3):
        for side, pattern in enumerate((LEFT, RIGHT)):
            hit = None
            for group, which in enumerate(pattern):
                if which == third:
                    here = lane // DIM == group
                    hit = here if hit is None else hit | here
            place_ref[third * LANES : (third + 1) * LANES, side * LANES : (side + 1) * LANES] = (same & hit).astype(BF16)
        place_ref[third * LANES : (third + 1) * LANES, 2 * LANES :] = (same & (lane < DIM)).astype(BF16)
    for copy in copies:
        copy.wait()
    n = points_ref.shape[1]
    spread_to = (iota((DIM, LANES), 1) % DIM == iota((DIM, LANES), 0)).astype(BF16)
    wide = None
    for part in split3(points_ref[...]):
        x = dot(part, spread_to, TN)
        wide = x if wide is None else wide + x
    wide = jnp.where(iota((n, LANES), 1) // DIM == iota((n, LANES), 0) % PER_ROW, wide, 0.0)
    block = jnp.concatenate([jnp.sum(wide[i : i + PER_ROW, :], axis=0, keepdims=True) for i in range(0, n, PER_ROW)], axis=0)
    table_ref[...] = jnp.concatenate([block] * (table_ref.shape[0] // block.shape[0]), axis=0)
    at = 0
    for ref in (first_ref, second_ref):
        count = ref.shape[1]
        ids_ref[:, at : at + count] = jnp.broadcast_to(ref[...], (SUB, count))
        ids = jnp.broadcast_to(ref[...].astype(F32), (LANES, count)).T.astype(jnp.int32)
        for t in range(0, table_ref.shape[0], LANES):
            select_ref[at : at + count, t : t + LANES] = (ids // PER_ROW == t + iota((count, LANES), 1)).astype(BF16)
        keep_ref[at : at + count, :] = (ids % PER_ROW == iota((count, LANES), 1) // DIM).astype(F32)
        at += count


def features_of(select, table, keep, place):
    n = select.shape[0]
    thirds = jnp.concatenate([(dot(select, part, NN) * keep).astype(BF16) for part in table], axis=1)
    both = dot(thirds, place, NN)
    x = both[:, 2 * LANES :]
    norm = jnp.sum(x * x, axis=1, keepdims=True)
    right = both[:, LANES : 2 * LANES]
    for i, part in enumerate(split3(jnp.broadcast_to(norm, (n, LANES)))):
        right = jnp.where(iota((n, LANES), 1) == NORM + i, part.astype(F32), right)
    return both[:, :LANES], right.astype(BF16), norm


def rbf(left, norm, right):
    n = left.shape[0]
    lane = iota((2 * SUB, LANES), 1)
    ones = ((lane >= NORM) & (lane < NORM + 3)).astype(BF16)
    lead = iota((n, LANES), 1) < DIM
    both = dot(jnp.concatenate([ones, jnp.where(lead, left, 0.0).astype(BF16), jnp.where(lead, 0.0, left).astype(BF16)], axis=0), right, NT)
    inner = both[2 * SUB : 2 * SUB + n] + both[2 * SUB + n :]
    return jnp.exp((norm + both[:1] - 2.0 * inner) * (-1.0 / DIM))


def row_of(tile, s):
    return jnp.broadcast_to(tile[s : s + 1, :], (SUB, LANES))


def spread(x):
    return jnp.broadcast_to(jnp.sum(x, axis=1, keepdims=True), (SUB, LANES))


def eliminate(rows, first_lane, more):
    sub = lax.broadcasted_iota(jnp.int32, (SUB, LANES), 0)
    lane = lax.broadcasted_iota(jnp.int32, (SUB, LANES), 1)
    at, off = first_lane // LANES, first_lane % LANES
    at2, off2 = (first_lane + BLOCK) // LANES, (first_lane + BLOCK) % LANES
    n_lt = len(rows[0])
    n_cur = BLOCK // SUB
    n_tiles = 2 * n_cur if more else n_cur
    cols = []
    for j in range(BLOCK):
        tiles = [spread(jnp.where(lane == off + j, rows[i][at], 0.0)) if i >= j // SUB else None for i in range(n_cur)]
        if more:
            row = row_of(rows[j // SUB][at2], j % SUB)
            tiles += [spread(jnp.where(lane == off2 + i * SUB + sub, row, 0.0)) for i in range(n_cur)]
        cols.append(tiles)
    own = (lane >= off) & (lane < off + BLOCK)
    rows = [list(r) for r in rows]
    for i in range(n_cur):
        rows[i][at] = jnp.where(own, (lane == off + i * SUB + sub).astype(F32), rows[i][at])
    if more:
        rows += [[jnp.zeros((SUB, LANES), F32) for _ in range(n_lt)] for _ in range(n_cur)]
    scaled = []
    for it in range(n_cur):
        shift = jnp.zeros((SUB, LANES), F32)
        scale = jnp.zeros((SUB, LANES), F32)
        for sl in range(0, SUB, 2):
            s = it * SUB + sl
            a = row_of(cols[s][it], sl)
            b = row_of(cols[s][it], sl + 1)
            c = row_of(cols[s + 1][it], sl + 1)
            det = a * c - b * b
            rdet = 1.0 / det
            ra = lax.rsqrt(a)
            ba = b * (ra * ra)
            rc = lax.rsqrt(c - b * ba)
            scale = jnp.where(sub == sl, ra, jnp.where(sub == sl + 1, rc, scale))
            shift = jnp.where(sub == sl + 1, ba, shift)
            begin = it if sl + 2 < SUB else it + 1
            m0, m1 = [None] * n_tiles, [None] * n_tiles
            for i in range(begin, n_tiles):
                u0, u1 = cols[s][i], cols[s + 1][i]
                m0[i] = (u0 * c - u1 * b) * rdet
                m1[i] = (u1 * a - u0 * b) * rdet
                if i == it:
                    m0[i] = jnp.where(sub > sl + 1, m0[i], 0.0)
                    m1[i] = jnp.where(sub > sl + 1, m1[i], 0.0)
            for j in range(s + 2, BLOCK):
                x0 = row_of(cols[s][j // SUB], j % SUB)
                x1 = row_of(cols[s + 1][j // SUB], j % SUB)
                for i in range(max(begin, j // SUB), n_tiles):
                    cols[j][i] = cols[j][i] - (m0[i] * x0 + m1[i] * x1)
            for t in range(n_lt):
                y0 = row_of(rows[it][t], sl)
                y1 = row_of(rows[it][t], sl + 1)
                for i in range(begin, n_tiles):
                    rows[i][t] = rows[i][t] - (m0[i] * y0 + m1[i] * y1)
        scaled.append([(r - shift * pltpu.roll(r, 1, 0)) * scale for r in rows[it]])
    return scaled, rows[n_cur:]


def inverse_factor(w_ref, x_refs, n, hooks):
    n_lt = n // LANES
    n_cur = BLOCK // SUB
    lane = iota((SUB, LANES), 1)

    def load(i, t):
        return w_ref[i * SUB : (i + 1) * SUB, t * LANES : (t + 1) * LANES]

    rows = [[load(i, t) for t in range(n_lt)] for i in range(n_cur)]
    for r in range(0, n, BLOCK):
        nxt = r + BLOCK
        at, off = r // LANES, r % LANES
        own = (lane >= off) & (lane < off + BLOCK)
        done, below = eliminate(rows, r, nxt < n)
        if nxt < n:
            rows = []
            for i in range(n_cur):
                tiles = [load(nxt // SUB + i, t) for t in range(n_lt)]
                tiles[at] = jnp.where(own, 0.0, tiles[at])
                rows.append([tile + more for tile, more in zip(tiles, below[i])])
        whole = jnp.concatenate([jnp.concatenate(t, axis=1) for t in done], axis=0)
        thirds = split3(whole)
        width = (at + 1) * LANES
        inside = iota((BLOCK, width), 1) < nxt
        for x_ref, part in zip(x_refs, thirds):
            x_ref[r:nxt, :width] = jnp.where(inside, part[:, :width].astype(F32), 0.0).astype(BF16)
        rest = nxt + BLOCK
        if rest < n:
            base = rest // LANES * LANES
            left = jnp.concatenate([thirds[i] for i in LEFT], axis=0)[:, base:].T
            right = jnp.concatenate([thirds[i] for i in RIGHT], axis=0)
            cuts = [rest, rest + BLOCK, n] if rest + BLOCK < n else [rest, n]
            for begin, end in zip(cuts, cuts[1:]):
                update = dot(left[begin - base : end - base, :], right, NN)
                wide = iota((end - begin, n), 1)
                w_ref[begin:end, :] = jnp.where((wide >= r) & (wide < nxt), 0.0, w_ref[begin:end, :]) - update
        for hook in hooks.get(nxt, ()):
            hook()


def per_device_kernel(
    table_ref, select_ref, keep_ref, ids_ref, place_ref, panels_out, schur_out,
    w_ref, x_refs, panels_ref, schur_ref, cols_right_ref, col_thirds, row_thirds, col_panel, row_panel, sems,
):
    n_rows, n_piv = panels_ref.shape
    cols_n = schur_ref.shape[1]
    chunk = row_thirds.shape[1]
    row_start = lax.axis_index("row") * n_rows
    col_start = lax.axis_index("col") * cols_n
    half = n_piv // 2
    place = place_ref[...]
    left, right, norm = features_of(select_ref[...], split3(table_ref[...]), keep_ref[...], place)
    own = iota((n_piv, n_piv), 0) == iota((n_piv, n_piv), 1)
    w_ref[...] = rbf(left, norm, right) + jnp.where(own, 0.1, 0.0)

    def run_features(start, count):
        rows = count // PER_ROW
        table = split3(table_ref[pl.ds(pl.multiple_of(start // PER_ROW, SUB), rows), :])
        select = (iota((count, rows), 0) // PER_ROW == iota((count, rows), 1)).astype(BF16)
        keep = (iota((count, LANES), 0) % PER_ROW == iota((count, LANES), 1) // DIM).astype(F32)
        return features_of(select, table, keep, place)

    def columns(out, at, start, count, side, norm):
        ids = start + iota((count, n_piv), 0)
        c = rbf(side, norm, right) + jnp.where(ids == ids_ref[:1, :], 0.1, 0.0)
        for i, part in enumerate(split3(c)):
            out[i, at : at + count, :] = part

    def col_columns():
        side, cols_right, norm = run_features(col_start, cols_n)
        cols_right_ref[...] = cols_right
        columns(col_thirds, 0, col_start, cols_n, side, norm)

    def row_columns(at, part, count):
        start = row_start + at + part
        side, _, norm = run_features(start, count)
        columns(row_thirds, part, start, count, side, norm)
        ids_row = start + iota((count, cols_n), 0)
        ids_col = col_start + iota((count, cols_n), 1)
        schur_ref[pl.ds(at + part, count), :] = rbf(side, norm, cols_right_ref[...]) + jnp.where(ids_row == ids_col, 0.1, 0.0)

    def panel_half(c_thirds, k):
        upto = (k + 1) * half
        return dot6([c_thirds[i, :, :upto] for i in range(3)], [x[k * half : upto, :upto] for x in x_refs], NT)

    def col_half(k):
        for i, part in enumerate(split3(panel_half(col_thirds, k))):
            col_panel[i, :, k * half : (k + 1) * half] = part

    def row_half(at, k):
        panel = panel_half(row_thirds, k)
        panels_ref[pl.ds(at, chunk), k * half : (k + 1) * half] = panel
        for i, part in enumerate(split3(panel)):
            row_panel[i, :, k * half : (k + 1) * half] = part

    def schur_half(at, k):
        here = slice(k * half, (k + 1) * half)
        low = dot6([row_panel[i, :, here] for i in range(3)], [col_panel[i, :, here] for i in range(3)], NT)
        schur_ref[pl.ds(at, chunk), :] = schur_ref[pl.ds(at, chunk), :] - low

    panel_copies = [
        pltpu.make_async_copy(
            panels_ref.at[:, k * half : (k + 1) * half], panels_out.at[:, k * half : (k + 1) * half], sems.at[k]
        )
        for k in range(2)
    ]
    schur_copy = pltpu.make_async_copy(schur_ref, schur_out, sems.at[2])
    if n_rows == chunk:
        q = chunk // 2
        hooks = {
            2 * BLOCK: [col_columns],
            4 * BLOCK: [lambda: row_columns(0, 0, q)],
            6 * BLOCK: [lambda: row_columns(0, q, q)],
            9 * BLOCK: [lambda: row_half(0, 0), panel_copies[0].start],
            11 * BLOCK: [lambda: col_half(0)],
            13 * BLOCK: [lambda: schur_half(0, 0)],
        }
        inverse_factor(w_ref, x_refs, n_piv, hooks)
        row_half(0, 1)
        panel_copies[1].start()
        col_half(1)
        schur_half(0, 1)
        schur_copy.start()
    else:
        inverse_factor(w_ref, x_refs, n_piv, {})
        col_columns()
        col_half(0)
        col_half(1)

        @pl.loop(0, n_rows // chunk)
        def _(i):
            at = pl.multiple_of(i * chunk, chunk)
            row_columns(at, 0, chunk)
            for k in range(2):
                row_half(at, k)
                schur_half(at, k)

        for copy in panel_copies:
            copy.start()
        schur_copy.start()
    for copy in panel_copies:
        copy.wait()
    schur_copy.wait()


def per_device(points, pivots_first, pivots_second):
    per_dev = points.shape[1]
    n_row = lax.axis_size("row")
    n_col = lax.axis_size("col")
    rows_n = per_dev * n_col
    cols_n = per_dev * n_row
    n_piv = pivots_first.shape[0] + pivots_second.shape[0]
    n_tab = n_row * n_col * per_dev * DIM // LANES
    vmem = pl.BlockSpec(memory_space=pltpu.VMEM)
    params = pltpu.CompilerParams(vmem_limit_bytes=VMEM_BYTES)
    copies, *found = pl.pallas_call(
        pack_kernel,
        out_shape=(
            jax.ShapeDtypeStruct((n_tab, LANES), F32),
            jax.ShapeDtypeStruct((n_piv, n_tab), BF16),
            jax.ShapeDtypeStruct((n_piv, LANES), F32),
            jax.ShapeDtypeStruct((SUB, n_piv), jnp.int32),
            jax.ShapeDtypeStruct((3 * LANES, 3 * LANES), BF16),
        ),
        in_specs=[pl.BlockSpec(memory_space=pltpu.HBM)] * 3,
        out_specs=(vmem,) * 5,
        scratch_shapes=[
            pltpu.VMEM((DIM, per_dev), F32),
            pltpu.VMEM((1, pivots_first.shape[0]), jnp.int32),
            pltpu.VMEM((1, pivots_second.shape[0]), jnp.int32),
            pltpu.SemaphoreType.DMA((3,)),
        ],
        compiler_params=params,
        name="pack",
    )(*(pltpu.with_memory_space_constraint(x, pltpu.HBM) for x in (points, pivots_first[None, :], pivots_second[None, :])))
    table = lax.all_to_all(copies, ("row", "col"), 0, 0, tiled=True)
    table, *found = lax.optimization_barrier((table, *found))
    chunk = min(rows_n, 256)
    return pl.pallas_call(
        per_device_kernel,
        out_shape=(jax.ShapeDtypeStruct((rows_n, n_piv), F32), jax.ShapeDtypeStruct((rows_n, cols_n), F32)),
        in_specs=[vmem] * 5,
        out_specs=(pl.BlockSpec(memory_space=pl.ANY),) * 2,
        scratch_shapes=[
            pltpu.VMEM((n_piv, n_piv), F32),
            [pltpu.VMEM((n_piv, n_piv), BF16)] * 3,
            pltpu.VMEM((rows_n, n_piv), F32),
            pltpu.VMEM((rows_n, cols_n), F32),
            pltpu.VMEM((cols_n, LANES), BF16),
            pltpu.VMEM((3, cols_n, n_piv), BF16),
            pltpu.VMEM((3, chunk, n_piv), BF16),
            pltpu.VMEM((3, cols_n, n_piv), BF16),
            pltpu.VMEM((3, chunk, n_piv), BF16),
            pltpu.SemaphoreType.DMA((3,)),
        ],
        compiler_params=params,
        name="pivoted_cholesky",
    )(table, *found)


def solution(mesh):
    return jax.shard_map(
        per_device,
        mesh=mesh,
        in_specs=(P(None, ("row", "col")), P(), P()),
        out_specs=(P("row", None), P("row", "col")),
        check_vma=False,
    )
```

time: 83.4 us -> 23.6 us (0.28)
  other arithmetic: 46.2 us -> 0 us
  blocking collectives: 27.1 us -> 14.5 us
  Pallas kernels: 0 us -> 8.21 us
  matrix products: 5.07 us -> 0 us
  local copies, waits for them, and re-layouts: 3.9 us -> 0 us
    another operation x10 -> x0, other arithmetic: 45.8 us -> none  [the longest x4 20.9 us: right_solve(): return jax.scipy.linalg.solve_triangular(root, columns.T, lower=True).T]
    all_gather x2 -> x0, blocking collectives: 27.1 us -> none  [the longest x1 16.3 us: per_device(): everything = lax.all_gather(row_pts, 'row', axis=1, tiled=True)]
    all_to_all x0 -> x1, blocking collectives: none -> 14.5 us  [per_device(): table = lax.all_to_all(copies, ('row', 'col'), 0, 0, tiled=True)]
    pallas_call x0 -> x2, Pallas kernels: none -> 8.21 us  [the longest x1 7.26 us: per_device(): pl.pallas_call(per_device_kernel, out_shape=(jax.ShapeDtypeStruct((rows_n...]
    dot_general x12 -> x0, matrix products: 3.61 us -> none  [the longest x8 2.32 us: kernel(): inner = jnp.dot(left.T, right, precision=lax.Precision.HIGHEST)]
    unnamed x9 -> x0, local copies, waits for them, and re-layouts: 2.89 us -> none
    another operation x5 -> x0, matrix products: 1.47 us -> none  [right_solve(): return jax.scipy.linalg.solve_triangular(root, columns.T, lower=True).T]
where the time goes in v3:
time: 23.6 us; the launch traced here: 23.4 us
  blocking collectives  14.5 us (61%)
  Pallas kernels  8.21 us (35%)
  between operations  0.64 us (3%)
    all_to_all x1, blocking collectives, per_device(): table = lax.all_to_all(copies, ('row', 'col'), 0, 0, tiled=True)  14.5 us
    pallas_call x1, Pallas kernels, per_device(): pl.pallas_call(per_device_kernel, out_shape=(jax.ShapeDtypeStruct((rows_n...  7.26 us
    pallas_call x1, Pallas kernels, per_device(): pl.pallas_call(pack_kernel, out_shape=(jax.ShapeDtypeStruct((n_tab, LANES...  0.95 us

profile of v3, /device:TPU:0, one launch (start us, length us, event | category | flops | bytes accessed | tf_op | source)
XLA Modules:
  0.0 23.4 jit_solution(11447695562011898428)
XLA Ops:
  0.6 0.9 %pack.1 = (f32[128,128]{1,0:T(8,128)S(1)}, bf16[256,128]{1,0:T(8,128)(2,1)S(1)}, f32[256,128]{1,0:T(8,128)S(1)}, s32[8,256]{1,0:T(8,128)S(1)}, bf16[384,384]{1,0:T(8,128)(2,1)S(1)}) custom-call(f32[16,32]{1,0:T(8,128)} %points_in.1, s32[1,128]{1,0:T(1,128)} %bitcast.6, s32[1,128]{1,0:T(1,128)} %bitcast.7), custom_call_target="tpu_custom_call" | custom-call | tf_op jit(solution)/shard_map/pack/pallas_call | solution.py:331
  1.6 14.5 %all_to_all.12 = f32[32,4,128]{2,1,0:T(4,128)S(1)} all-to-all(f32[32,4,128]{2,1,0:T(4,128)S(1)} %bitcast.5), channel_id=1, replica_groups=mesh['row'=4,'col'=8] {'row','col'}, dimensions={0} | all-to-all | bytes 131072 | tf_op jit(solution)/shard_map/all_to_all | solution.py:351
  16.1 7.3 %pivoted_cholesky.1 = (f32[256,256]{1,0:T(8,128)}, f32[256,128]{1,0:T(8,128)}) custom-call(f32[128,128]{1,0:T(8,128)S(1)} %bitcast.4, bf16[256,128]{1,0:T(8,128)(2,1)S(1)} %get-tuple-element.18.select_ref, f32[256,128]{1,0:T(8,128)S(1)} %get-tuple-element.19.keep_ref, s32[8,256]{1,0:T(8,128)S(1)} %get-tuple-element.20.ids_ref, ...), custom_call_target="tpu_custom_call" | custom-call | tf_op jit(solution)/shard_map/pivoted_cholesky/pallas_call | solution.py:354

commit v4 on v3

--- a/solution.py
+++ b/solution.py
@@ -38,9 +38,15 @@
     return hi, mid, (rest - mid.astype(F32)).astype(BF16)
 
 
-def dot6(a, b, dims):
-    p = [dot(a[i], b[j], dims) for i, j in zip(LEFT, RIGHT)]
-    return p[0] + ((p[1] + p[2]) + ((p[3] + p[4]) + p[5]))
+def dot6(a, b):
+    n = b[0].shape[0]
+    wide = dot(
+        jnp.concatenate([a[0], a[1]], axis=1),
+        jnp.concatenate([jnp.concatenate([b[0], b[0]], axis=1), jnp.concatenate([b[1], b[1]], axis=1)], axis=0),
+        NT,
+    )
+    rest = dot(jnp.concatenate([a[0], a[2]], axis=1), jnp.concatenate([b[2], b[0]], axis=1), NT)
+    return wide[:, :n] + (wide[:, n:] + rest)
 
 
 def pack_kernel(points_in, first_in, second_in, table_ref, select_ref, keep_ref, ids_ref, place_ref, points_ref, first_ref, second_ref, sems):
@@ -121,13 +127,13 @@
     n_lt = len(rows[0])
     n_cur = BLOCK // SUB
     n_tiles = 2 * n_cur if more else n_cur
-    cols = []
-    for j in range(BLOCK):
-        tiles = [spread(jnp.where(lane == off + j, rows[i][at], 0.0)) if i >= j // SUB else None for i in range(n_cur)]
-        if more:
+    cols = [
+        [spread(jnp.where(lane == off + j, rows[i][at], 0.0)) if i >= j // SUB else None for i in range(n_cur)] for j in range(BLOCK)
+    ]
+    if more:
+        for j in range(BLOCK):
             row = row_of(rows[j // SUB][at2], j % SUB)
-            tiles += [spread(jnp.where(lane == off2 + i * SUB + sub, row, 0.0)) for i in range(n_cur)]
-        cols.append(tiles)
+            cols[j] += [spread(jnp.where(lane == off2 + i * SUB + sub, row, 0.0)) for i in range(n_cur)]
     own = (lane >= off) & (lane < off + BLOCK)
     rows = [list(r) for r in rows]
     for i in range(n_cur):
@@ -256,7 +262,7 @@
 
     def panel_half(c_thirds, k):
         upto = (k + 1) * half
-        return dot6([c_thirds[i, :, :upto] for i in range(3)], [x[k * half : upto, :upto] for x in x_refs], NT)
+        return dot6([c_thirds[i, :, :upto] for i in range(3)], [x[k * half : upto, :upto] for x in x_refs])
 
     def col_half(k):
         for i, part in enumerate(split3(panel_half(col_thirds, k))):
@@ -270,7 +276,7 @@
 
     def schur_half(at, k):
         here = slice(k * half, (k + 1) * half)
-        low = dot6([row_panel[i, :, here] for i in range(3)], [col_panel[i, :, here] for i in range(3)], NT)
+        low = dot6([row_panel[i, :, here] for i in range(3)], [col_panel[i, :, here] for i in range(3)])
         schur_ref[pl.ds(at, chunk), :] = schur_ref[pl.ds(at, chunk), :] - low
 
     panel_copies = [

time: 23.6 us -> 23.4 us (level)
  no operation moved by 1% of the time
where the time goes in v4:
time: 23.4 us; the launch traced here: 23.2 us
  blocking collectives  14.5 us (62%)
  Pallas kernels  8.02 us (34%)
  between operations  0.64 us (3%)
    all_to_all x1, blocking collectives, per_device(): table = lax.all_to_all(copies, ('row', 'col'), 0, 0, tiled=True)  14.5 us
    pallas_call x1, Pallas kernels, per_device(): pl.pallas_call(per_device_kernel, out_shape=(jax.ShapeDtypeStruct((rows_n...  7.07 us
    pallas_call x1, Pallas kernels, per_device(): pl.pallas_call(pack_kernel, out_shape=(jax.ShapeDtypeStruct((n_tab, LANES...  0.95 us

profile of v4, /device:TPU:0, one launch (start us, length us, event | category | flops | bytes accessed | tf_op | source)
XLA Modules:
  0.0 23.2 jit_solution(9164172473281193280)
XLA Ops:
  0.6 0.9 %pack.1 = (f32[128,128]{1,0:T(8,128)S(1)}, bf16[256,128]{1,0:T(8,128)(2,1)S(1)}, f32[256,128]{1,0:T(8,128)S(1)}, s32[8,256]{1,0:T(8,128)S(1)}, bf16[384,384]{1,0:T(8,128)(2,1)S(1)}) custom-call(f32[16,32]{1,0:T(8,128)} %points_in.1, s32[1,128]{1,0:T(1,128)} %bitcast.6, s32[1,128]{1,0:T(1,128)} %bitcast.7), custom_call_target="tpu_custom_call" | custom-call | tf_op jit(solution)/shard_map/pack/pallas_call | solution.py:337
  1.6 14.5 %all_to_all.12 = f32[32,4,128]{2,1,0:T(4,128)S(1)} all-to-all(f32[32,4,128]{2,1,0:T(4,128)S(1)} %bitcast.5), channel_id=1, replica_groups=mesh['row'=4,'col'=8] {'row','col'}, dimensions={0} | all-to-all | bytes 131072 | tf_op jit(solution)/shard_map/all_to_all | solution.py:357
  16.1 7.1 %pivoted_cholesky.1 = (f32[256,256]{1,0:T(8,128)}, f32[256,128]{1,0:T(8,128)}) custom-call(f32[128,128]{1,0:T(8,128)S(1)} %bitcast.4, bf16[256,128]{1,0:T(8,128)(2,1)S(1)} %get-tuple-element.18.select_ref, f32[256,128]{1,0:T(8,128)S(1)} %get-tuple-element.19.keep_ref, s32[8,256]{1,0:T(8,128)S(1)} %get-tuple-element.20.ids_ref, ...), custom_call_target="tpu_custom_call" | custom-call | tf_op jit(solution)/shard_map/pivoted_cholesky/pallas_call | solution.py:360

commit v5 on v4

--- a/solution.py
+++ b/solution.py
@@ -221,7 +221,8 @@
 
 def per_device_kernel(
     table_ref, select_ref, keep_ref, ids_ref, place_ref, panels_out, schur_out,
-    w_ref, x_refs, panels_ref, schur_ref, cols_right_ref, col_thirds, row_thirds, col_panel, row_panel, sems,
+    w_refs, x_refs, between_ref, panels_ref, schur_ref, cols_right_ref, col_thirds, row_thirds, col_second, row_second,
+    col_panel, row_panel, sems,
 ):
     n_rows, n_piv = panels_ref.shape
     cols_n = schur_ref.shape[1]
@@ -231,8 +232,26 @@
     half = n_piv // 2
     place = place_ref[...]
     left, right, norm = features_of(select_ref[...], split3(table_ref[...]), keep_ref[...], place)
-    own = iota((n_piv, n_piv), 0) == iota((n_piv, n_piv), 1)
-    w_ref[...] = rbf(left, norm, right) + jnp.where(own, 0.1, 0.0)
+    own = jnp.where(iota((half, half), 0) == iota((half, half), 1), 0.1, 0.0)
+    w_refs[0][...] = rbf(left[:half], norm[:half], right[:half]) + own
+
+    def of(ref, k):
+        return [ref[i, :, k * half : (k + 1) * half] for i in range(3)]
+
+    def keep_thirds(ref, k, value):
+        for i, part in enumerate(split3(value)):
+            ref[i, :, k * half : (k + 1) * half] = part
+
+    def second_pivots():
+        k = rbf(left[half:], norm[half:], right)
+        keep_thirds(between_ref, 0, k[:, :half])
+        w_refs[1][...] = k[:, half:] + own
+
+    def second_block():
+        between = split3(dot6(of(between_ref, 0), [x[...] for x in x_refs[:3]]))
+        for i, part in enumerate(between):
+            between_ref[i] = part
+        w_refs[1][...] = w_refs[1][...] - dot6(between, between)
 
     def run_features(start, count):
         rows = count // PER_ROW
@@ -241,43 +260,40 @@
         keep = (iota((count, LANES), 0) % PER_ROW == iota((count, LANES), 1) // DIM).astype(F32)
         return features_of(select, table, keep, place)
 
-    def columns(out, at, start, count, side, norm):
+    def columns(thirds, second, at, start, count, side, norm):
         ids = start + iota((count, n_piv), 0)
         c = rbf(side, norm, right) + jnp.where(ids == ids_ref[:1, :], 0.1, 0.0)
-        for i, part in enumerate(split3(c)):
-            out[i, at : at + count, :] = part
+        for i, part in enumerate(split3(c[:, :half])):
+            thirds[i, at : at + count, :half] = part
+        second[at : at + count, :] = c[:, half:]
 
     def col_columns():
         side, cols_right, norm = run_features(col_start, cols_n)
         cols_right_ref[...] = cols_right
-        columns(col_thirds, 0, col_start, cols_n, side, norm)
+        columns(col_thirds, col_second, 0, col_start, cols_n, side, norm)
 
     def row_columns(at, part, count):
         start = row_start + at + part
         side, _, norm = run_features(start, count)
-        columns(row_thirds, part, start, count, side, norm)
+        columns(row_thirds, row_second, part, start, count, side, norm)
         ids_row = start + iota((count, cols_n), 0)
         ids_col = col_start + iota((count, cols_n), 1)
         schur_ref[pl.ds(at + part, count), :] = rbf(side, norm, cols_right_ref[...]) + jnp.where(ids_row == ids_col, 0.1, 0.0)
 
-    def panel_half(c_thirds, k):
-        upto = (k + 1) * half
-        return dot6([c_thirds[i, :, :upto] for i in range(3)], [x[k * half : upto, :upto] for x in x_refs])
-
     def col_half(k):
-        for i, part in enumerate(split3(panel_half(col_thirds, k))):
-            col_panel[i, :, k * half : (k + 1) * half] = part
+        keep_thirds(col_panel, k, dot6(of(col_thirds, k), [x[...] for x in x_refs[3 * k : 3 * k + 3]]))
 
     def row_half(at, k):
-        panel = panel_half(row_thirds, k)
+        panel = dot6(of(row_thirds, k), [x[...] for x in x_refs[3 * k : 3 * k + 3]])
         panels_ref[pl.ds(at, chunk), k * half : (k + 1) * half] = panel
-        for i, part in enumerate(split3(panel)):
-            row_panel[i, :, k * half : (k + 1) * half] = part
+        keep_thirds(row_panel, k, panel)
+
+    def second_columns(thirds, second, panel):
+        between = [between_ref[i] for i in range(3)]
+        keep_thirds(thirds, 1, second[...] - dot6(of(panel, 0), between))
 
     def schur_half(at, k):
-        here = slice(k * half, (k + 1) * half)
-        low = dot6([row_panel[i, :, here] for i in range(3)], [col_panel[i, :, here] for i in range(3)])
-        schur_ref[pl.ds(at, chunk), :] = schur_ref[pl.ds(at, chunk), :] - low
+        schur_ref[pl.ds(at, chunk), :] = schur_ref[pl.ds(at, chunk), :] - dot6(of(row_panel, k), of(col_panel, k))
 
     panel_copies = [
         pltpu.make_async_copy(
@@ -288,32 +304,35 @@
     schur_copy = pltpu.make_async_copy(schur_ref, schur_out, sems.at[2])
     if n_rows == chunk:
         q = chunk // 2
-        hooks = {
-            2 * BLOCK: [col_columns],
-            4 * BLOCK: [lambda: row_columns(0, 0, q)],
-            6 * BLOCK: [lambda: row_columns(0, q, q)],
-            9 * BLOCK: [lambda: row_half(0, 0), panel_copies[0].start],
-            11 * BLOCK: [lambda: col_half(0)],
-            13 * BLOCK: [lambda: schur_half(0, 0)],
-        }
-        inverse_factor(w_ref, x_refs, n_piv, hooks)
+        first = {2 * BLOCK: [second_pivots], 4 * BLOCK: [col_columns]}
+        inverse_factor(w_refs[0], x_refs[:3], half, first)
+        second_block()
+        row_columns(0, 0, chunk)
+        second = {1 * BLOCK: [lambda: row_half(0, 0), panel_copies[0].start], 2 * BLOCK: [lambda: col_half(0)], 3 * BLOCK: [lambda: second_columns(row_thirds, row_second, row_panel)], 5 * BLOCK: [lambda: second_columns(col_thirds, col_second, col_panel)], 6 * BLOCK: [lambda: schur_half(0, 0)]}
+        inverse_factor(w_refs[1], x_refs[3:], half, second)
         row_half(0, 1)
         panel_copies[1].start()
         col_half(1)
         schur_half(0, 1)
         schur_copy.start()
     else:
-        inverse_factor(w_ref, x_refs, n_piv, {})
+        inverse_factor(w_refs[0], x_refs[:3], half, {})
+        second_pivots()
+        second_block()
+        inverse_factor(w_refs[1], x_refs[3:], half, {})
         col_columns()
         col_half(0)
+        second_columns(col_thirds, col_second, col_panel)
         col_half(1)
 
         @pl.loop(0, n_rows // chunk)
         def _(i):
             at = pl.multiple_of(i * chunk, chunk)
             row_columns(at, 0, chunk)
+            row_half(at, 0)
+            second_columns(row_thirds, row_second, row_panel)
+            row_half(at, 1)
             for k in range(2):
-                row_half(at, k)
                 schur_half(at, k)
 
         for copy in panel_copies:
@@ -357,19 +376,23 @@
     table = lax.all_to_all(copies, ("row", "col"), 0, 0, tiled=True)
     table, *found = lax.optimization_barrier((table, *found))
     chunk = min(rows_n, 256)
+    half = n_piv // 2
     return pl.pallas_call(
         per_device_kernel,
         out_shape=(jax.ShapeDtypeStruct((rows_n, n_piv), F32), jax.ShapeDtypeStruct((rows_n, cols_n), F32)),
         in_specs=[vmem] * 5,
         out_specs=(pl.BlockSpec(memory_space=pl.ANY),) * 2,
         scratch_shapes=[
-            pltpu.VMEM((n_piv, n_piv), F32),
-            [pltpu.VMEM((n_piv, n_piv), BF16)] * 3,
+            [pltpu.VMEM((half, half), F32)] * 2,
+            [pltpu.VMEM((half, half), BF16)] * 6,
+            pltpu.VMEM((3, half, half), BF16),
             pltpu.VMEM((rows_n, n_piv), F32),
             pltpu.VMEM((rows_n, cols_n), F32),
             pltpu.VMEM((cols_n, LANES), BF16),
             pltpu.VMEM((3, cols_n, n_piv), BF16),
             pltpu.VMEM((3, chunk, n_piv), BF16),
+            pltpu.VMEM((cols_n, half), F32),
+            pltpu.VMEM((chunk, half), F32),
             pltpu.VMEM((3, cols_n, n_piv), BF16),
             pltpu.VMEM((3, chunk, n_piv), BF16),
             pltpu.SemaphoreType.DMA((3,)),

time: 23.4 us -> 23 us (0.983)
  Pallas kernels: 8.02 us -> 7.61 us
    pallas_call x1, Pallas kernels: 7.07 us -> 6.66 us  [per_device(): pl.pallas_call(per_device_kernel, out_shape=(jax.ShapeDtypeStruct((rows_n...]
where the time goes in v5:
time: 23 us; the launch traced here: 22.8 us
  blocking collectives  14.5 us (63%)
  Pallas kernels  7.61 us (33%)
  between operations  0.64 us (3%)
    all_to_all x1, blocking collectives, per_device(): table = lax.all_to_all(copies, ('row', 'col'), 0, 0, tiled=True)  14.5 us
    pallas_call x1, Pallas kernels, per_device(): pl.pallas_call(per_device_kernel, out_shape=(jax.ShapeDtypeStruct((rows_n...  6.66 us
    pallas_call x1, Pallas kernels, per_device(): pl.pallas_call(pack_kernel, out_shape=(jax.ShapeDtypeStruct((n_tab, LANES...  0.95 us

profile of v5, /device:TPU:0, one launch (start us, length us, event | category | flops | bytes accessed | tf_op | source)
XLA Modules:
  0.0 22.8 jit_solution(7157466964666714439)
XLA Ops:
  0.6 0.9 %pack.1 = (f32[128,128]{1,0:T(8,128)S(1)}, bf16[256,128]{1,0:T(8,128)(2,1)S(1)}, f32[256,128]{1,0:T(8,128)S(1)}, s32[8,256]{1,0:T(8,128)S(1)}, bf16[384,384]{1,0:T(8,128)(2,1)S(1)}) custom-call(f32[16,32]{1,0:T(8,128)} %points_in.1, s32[1,128]{1,0:T(1,128)} %bitcast.6, s32[1,128]{1,0:T(1,128)} %bitcast.7), custom_call_target="tpu_custom_call" | custom-call | tf_op jit(solution)/shard_map/pack/pallas_call | solution.py:356
  1.6 14.5 %all_to_all.12 = f32[32,4,128]{2,1,0:T(4,128)S(1)} all-to-all(f32[32,4,128]{2,1,0:T(4,128)S(1)} %bitcast.5), channel_id=1, replica_groups=mesh['row'=4,'col'=8] {'row','col'}, dimensions={0} | all-to-all | bytes 131072 | tf_op jit(solution)/shard_map/all_to_all | solution.py:376
  16.1 6.7 %pivoted_cholesky.1 = (f32[256,256]{1,0:T(8,128)}, f32[256,128]{1,0:T(8,128)}) custom-call(f32[128,128]{1,0:T(8,128)S(1)} %bitcast.4, bf16[256,128]{1,0:T(8,128)(2,1)S(1)} %get-tuple-element.18.select_ref, f32[256,128]{1,0:T(8,128)S(1)} %get-tuple-element.19.keep_ref, s32[8,256]{1,0:T(8,128)S(1)} %get-tuple-element.20.ids_ref, ...), custom_call_target="tpu_custom_call" | custom-call | tf_op jit(solution)/shard_map/pivoted_cholesky/pallas_call | solution.py:380

commit v6 on v5

--- a/solution.py
+++ b/solution.py
@@ -70,13 +70,13 @@
     for copy in copies:
         copy.wait()
     n = points_ref.shape[1]
-    spread_to = (iota((DIM, LANES), 1) % DIM == iota((DIM, LANES), 0)).astype(BF16)
-    wide = None
-    for part in split3(points_ref[...]):
-        x = dot(part, spread_to, TN)
-        wide = x if wide is None else wide + x
-    wide = jnp.where(iota((n, LANES), 1) // DIM == iota((n, LANES), 0) % PER_ROW, wide, 0.0)
-    block = jnp.concatenate([jnp.sum(wide[i : i + PER_ROW, :], axis=0, keepdims=True) for i in range(0, n, PER_ROW)], axis=0)
+    tall = jnp.concatenate([points_ref[...], jnp.zeros((DIM, LANES - n), F32)], axis=1)
+    tall = jnp.concatenate([tall, jnp.zeros((LANES - DIM, LANES), F32)], axis=0).T
+    block = []
+    for i in range(0, n, PER_ROW):
+        moved = pltpu.roll(tall[i : i + PER_ROW, :], 0, 1, stride=DIM, stride_axis=0)
+        block.append(jnp.sum(moved, axis=0, keepdims=True))
+    block = jnp.concatenate(block, axis=0)
     table_ref[...] = jnp.concatenate([block] * (table_ref.shape[0] // block.shape[0]), axis=0)
     at = 0
     for ref in (first_ref, second_ref):
@@ -130,18 +130,25 @@
     cols = [
         [spread(jnp.where(lane == off + j, rows[i][at], 0.0)) if i >= j // SUB else None for i in range(n_cur)] for j in range(BLOCK)
     ]
+
+    def add_below(it):
+        for j in range(it * SUB, (it + 1) * SUB):
+            row = row_of(rows[it][at2], j % SUB)
+            cols[j] += [spread(jnp.where(lane == off2 + i * SUB + sub, row, 0.0)) for i in range(n_cur)]
+
     if more:
-        for j in range(BLOCK):
-            row = row_of(rows[j // SUB][at2], j % SUB)
-            cols[j] += [spread(jnp.where(lane == off2 + i * SUB + sub, row, 0.0)) for i in range(n_cur)]
-    own = (lane >= off) & (lane < off + BLOCK)
+        add_below(0)
     rows = [list(r) for r in rows]
-    for i in range(n_cur):
-        rows[i][at] = jnp.where(own, (lane == off + i * SUB + sub).astype(F32), rows[i][at])
     if more:
         rows += [[jnp.zeros((SUB, LANES), F32) for _ in range(n_lt)] for _ in range(n_cur)]
     scaled = []
     for it in range(n_cur):
+        if more and it > 0:
+            add_below(it)
+        own = (lane >= off + it * SUB) & (lane < off + (it + 1) * SUB)
+        for i in range(it, n_tiles):
+            unit = (lane == off + i * SUB + sub).astype(F32) if i == it else jnp.zeros((SUB, LANES), F32)
+            rows[i][at] = jnp.where(own, unit, rows[i][at])
         shift = jnp.zeros((SUB, LANES), F32)
         scale = jnp.zeros((SUB, LANES), F32)
         for sl in range(0, SUB, 2):
@@ -168,7 +175,7 @@
             for j in range(s + 2, BLOCK):
                 x0 = row_of(cols[s][j // SUB], j % SUB)
                 x1 = row_of(cols[s + 1][j // SUB], j % SUB)
-                for i in range(max(begin, j // SUB), n_tiles):
+                for i in range(max(begin, j // SUB), len(cols[j])):
                     cols[j][i] = cols[j][i] - (m0[i] * x0 + m1[i] * x1)
             for t in range(n_lt):
                 y0 = row_of(rows[it][t], sl)
@@ -176,6 +183,9 @@
                 for i in range(begin, n_tiles):
                     rows[i][t] = rows[i][t] - (m0[i] * y0 + m1[i] * y1)
         scaled.append([(r - shift * pltpu.roll(r, 1, 0)) * scale for r in rows[it]])
+        later = (lane >= off + (it + 1) * SUB) & (lane < off + BLOCK)
+        if it + 1 < n_cur:
+            scaled[it][at] = jnp.where(later, 0.0, scaled[it][at])
     return scaled, rows[n_cur:]
 
 
@@ -310,10 +320,12 @@
         row_columns(0, 0, chunk)
         second = {1 * BLOCK: [lambda: row_half(0, 0), panel_copies[0].start], 2 * BLOCK: [lambda: col_half(0)], 3 * BLOCK: [lambda: second_columns(row_thirds, row_second, row_panel)], 5 * BLOCK: [lambda: second_columns(col_thirds, col_second, col_panel)], 6 * BLOCK: [lambda: schur_half(0, 0)]}
         inverse_factor(w_refs[1], x_refs[3:], half, second)
-        row_half(0, 1)
+        last = [jnp.concatenate([r, c], axis=0) for r, c in zip(of(row_thirds, 1), of(col_thirds, 1))]
+        both = dot6(last, [x[...] for x in x_refs[3:]])
+        panels_ref[:, half:] = both[:chunk]
         panel_copies[1].start()
-        col_half(1)
-        schur_half(0, 1)
+        both = split3(both)
+        schur_ref[...] = schur_ref[...] - dot6([p[:chunk] for p in both], [p[chunk:] for p in both])
         schur_copy.start()
     else:
         inverse_factor(w_refs[0], x_refs[:3], half, {})

time: 23 us -> 23 us (level)
  no operation moved by 1% of the time
where the time goes in v6:
time: 23 us; the launch traced here: 22.8 us
  blocking collectives  14.5 us (63%)
  Pallas kernels  7.58 us (33%)
  between operations  0.64 us (3%)
    all_to_all x1, blocking collectives, per_device(): table = lax.all_to_all(copies, ('row', 'col'), 0, 0, tiled=True)  14.5 us
    pallas_call x1, Pallas kernels, per_device(): pl.pallas_call(per_device_kernel, out_shape=(jax.ShapeDtypeStruct((rows_n...  6.65 us
    pallas_call x1, Pallas kernels, per_device(): pl.pallas_call(pack_kernel, out_shape=(jax.ShapeDtypeStruct((n_tab, LANES...  0.93 us

profile of v6, /device:TPU:0, one launch (start us, length us, event | category | flops | bytes accessed | tf_op | source)
XLA Modules:
  0.0 22.8 jit_solution(544951954198885256)
XLA Ops:
  0.6 0.9 %pack.1 = (f32[128,128]{1,0:T(8,128)S(1)}, bf16[256,128]{1,0:T(8,128)(2,1)S(1)}, f32[256,128]{1,0:T(8,128)S(1)}, s32[8,256]{1,0:T(8,128)S(1)}, bf16[384,384]{1,0:T(8,128)(2,1)S(1)}) custom-call(f32[16,32]{1,0:T(8,128)} %points_in.1, s32[1,128]{1,0:T(1,128)} %bitcast.6, s32[1,128]{1,0:T(1,128)} %bitcast.7), custom_call_target="tpu_custom_call" | custom-call | tf_op jit(solution)/shard_map/pack/pallas_call | solution.py:368
  1.6 14.5 %all_to_all.12 = f32[32,4,128]{2,1,0:T(4,128)S(1)} all-to-all(f32[32,4,128]{2,1,0:T(4,128)S(1)} %bitcast.5), channel_id=1, replica_groups=mesh['row'=4,'col'=8] {'row','col'}, dimensions={0} | all-to-all | bytes 131072 | tf_op jit(solution)/shard_map/all_to_all | solution.py:388
  16.1 6.6 %pivoted_cholesky.1 = (f32[256,256]{1,0:T(8,128)}, f32[256,128]{1,0:T(8,128)}) custom-call(f32[128,128]{1,0:T(8,128)S(1)} %bitcast.4, bf16[256,128]{1,0:T(8,128)(2,1)S(1)} %get-tuple-element.18.select_ref, f32[256,128]{1,0:T(8,128)S(1)} %get-tuple-element.19.keep_ref, s32[8,256]{1,0:T(8,128)S(1)} %get-tuple-element.20.ids_ref, ...), custom_call_target="tpu_custom_call" | custom-call | tf_op jit(solution)/shard_map/pivoted_cholesky/pallas_call | solution.py:392

commit v7 on v6

--- a/solution.py
+++ b/solution.py
@@ -165,10 +165,15 @@
             shift = jnp.where(sub == sl + 1, ba, shift)
             begin = it if sl + 2 < SUB else it + 1
             m0, m1 = [None] * n_tiles, [None] * n_tiles
+            ar, br, cr = a * rdet, b * rdet, c * rdet
             for i in range(begin, n_tiles):
                 u0, u1 = cols[s][i], cols[s + 1][i]
-                m0[i] = (u0 * c - u1 * b) * rdet
-                m1[i] = (u1 * a - u0 * b) * rdet
+                if i == it:
+                    m0[i] = (u0 * c - u1 * b) * rdet
+                    m1[i] = (u1 * a - u0 * b) * rdet
+                else:
+                    m0[i] = u0 * cr - u1 * br
+                    m1[i] = u1 * ar - u0 * br
                 if i == it:
                     m0[i] = jnp.where(sub > sl + 1, m0[i], 0.0)
                     m1[i] = jnp.where(sub > sl + 1, m1[i], 0.0)

time: 23 us -> 23 us (level)
  no operation moved by 1% of the time
where the time goes in v7:
time: 23 us; the launch traced here: 22.8 us
  blocking collectives  14.5 us (63%)
  Pallas kernels  7.59 us (33%)
  between operations  0.64 us (3%)
    all_to_all x1, blocking collectives, per_device(): table = lax.all_to_all(copies, ('row', 'col'), 0, 0, tiled=True)  14.5 us
    pallas_call x1, Pallas kernels, per_device(): pl.pallas_call(per_device_kernel, out_shape=(jax.ShapeDtypeStruct((rows_n...  6.65 us
    pallas_call x1, Pallas kernels, per_device(): pl.pallas_call(pack_kernel, out_shape=(jax.ShapeDtypeStruct((n_tab, LANES...  0.93 us

profile of v7, /device:TPU:0, one launch (start us, length us, event | category | flops | bytes accessed | tf_op | source)
XLA Modules:
  0.0 22.8 jit_solution(3754661368491935798)
XLA Ops:
  0.6 0.9 %pack.1 = (f32[128,128]{1,0:T(8,128)S(1)}, bf16[256,128]{1,0:T(8,128)(2,1)S(1)}, f32[256,128]{1,0:T(8,128)S(1)}, s32[8,256]{1,0:T(8,128)S(1)}, bf16[384,384]{1,0:T(8,128)(2,1)S(1)}) custom-call(f32[16,32]{1,0:T(8,128)} %points_in.1, s32[1,128]{1,0:T(1,128)} %bitcast.6, s32[1,128]{1,0:T(1,128)} %bitcast.7), custom_call_target="tpu_custom_call" | custom-call | tf_op jit(solution)/shard_map/pack/pallas_call | solution.py:373
  1.6 14.5 %all_to_all.12 = f32[32,4,128]{2,1,0:T(4,128)S(1)} all-to-all(f32[32,4,128]{2,1,0:T(4,128)S(1)} %bitcast.5), channel_id=1, replica_groups=mesh['row'=4,'col'=8] {'row','col'}, dimensions={0} | all-to-all | bytes 131072 | tf_op jit(solution)/shard_map/all_to_all | solution.py:393
  16.1 6.7 %pivoted_cholesky.1 = (f32[256,256]{1,0:T(8,128)}, f32[256,128]{1,0:T(8,128)}) custom-call(f32[128,128]{1,0:T(8,128)S(1)} %bitcast.4, bf16[256,128]{1,0:T(8,128)(2,1)S(1)} %get-tuple-element.18.select_ref, f32[256,128]{1,0:T(8,128)S(1)} %get-tuple-element.19.keep_ref, s32[8,256]{1,0:T(8,128)S(1)} %get-tuple-element.20.ids_ref, ...), custom_call_target="tpu_custom_call" | custom-call | tf_op jit(solution)/shard_map/pivoted_cholesky/pallas_call | solution.py:397
